TPU v7x, 128 devices: a whole 4x4x4 slice. The times are simulated.
128 devices in a mesh: tgt: 16 (over z, x), src: 8 (over y, core).
Axes of the slice: x: 4, y: 4, z: 4, core: 2. Of those that a mesh axis runs over, the one named last changes fastest.
Arguments:
- points: bfloat16 [262144, 256], P(('tgt', 'src')), may hold values from -0.4 to 0.4
- weights: bfloat16 [262144, 64], P(('tgt', 'src')), may hold values from -6 to 6
- near_list: int32 [2048, 16], P(('tgt', 'src')), may hold values from -1 to 127, as said below
- far_list: int32 [2048, 3, 8], P('tgt', None, 'src'), may hold values from -1 to 63, as said below
- skel_index: int32 [896, 256], P(('tgt', 'src')), may hold values from 0 to 2047, as said below
- equiv_weights: bfloat16 [896, 256, 64], P(('tgt', 'src')), may hold values from -6 to 6
Outputs:
- potential: float32 [262144, 64], P(('tgt', 'src'))
Inputs may be any that keep to these rules, and one draw needn't show every extreme that they name: `near_list`: row b lists blocks of b's group of 128 blocks by their index within the group: first b itself, then distinct other blocks; after a row's live entries all are -1; every row has 4 or more live entries. `far_list`: entry [b, l, c] is -1 or a level-l node owned by a device of src index c, numbered as the owner's tgt index times (16 // (4 * 2 ** l)) plus the node's number among the owner's level-l nodes. `skel_index`: Level-l nodes of a device cover 4 * 128 * 2 ** l consecutive points of that device each, in order; a node's 256 entries are increasing indices of the device's points inside the node.
All inputs are finite; a program needn't handle non-finite values.
Results may differ from a plain program's by a relative error of at most 0.0023.
Values may be sent and summed in bfloat16 or wider, within the bound.
No kernel may reach another device: no remote copies, remote signals or barrier semaphores. Data moves between devices by JAX's collectives and lax.ppermute only.
A program may use at most 192 MiB of HBM per device.

v0:
```python
import jax
import jax.numpy as jnp
from jax import lax
from jax.sharding import PartitionSpec as P

E = 256
WCOL = 64
BLK = 128
RANK = 256
NEAR = 16
LEVELS = 3
kernel_rate = 2.0


def square_norms(values):
    return jnp.sum(jnp.square(values.astype(jnp.float32)), axis=-1)


def tile_kernel(targets, target_norms, sources, source_norms, live_mask):
    dot_terms = jnp.einsum("bie,bse->bis", targets, sources, preferred_element_type=jnp.float32)
    sq_dist = target_norms[:, :, None] + source_norms[:, None, :] - 2.0 * dot_terms
    return jnp.where(live_mask[:, None, :], jnp.exp(-kernel_rate * sq_dist), 0.0).astype(
        jnp.bfloat16
    )


def apply_tile(kernel, source_weights):
    return jnp.einsum("bis,bsw->biw", kernel, source_weights, preferred_element_type=jnp.float32)


def shards(points, weights, near_list, far_list, skel_index, equiv_weights):
    point_dev = points.shape[0]
    blk_dev = point_dev // BLK
    src_size = lax.axis_size("src")
    src_index = lax.axis_index("src")
    group_blocks = src_size * blk_dev
    node_dev = skel_index.shape[0]
    level_nodes = [blk_dev // (4 * 2**tree_level) for tree_level in range(LEVELS)]
    level_start = [sum(level_nodes[:tree_level]) for tree_level in range(LEVELS)]
    group_pts, group_wts = (
        lax.all_gather(points, "src", axis=0, tiled=True),
        lax.all_gather(weights, "src", axis=0, tiled=True),
    )
    tgt_blocks = group_pts.reshape(group_blocks, BLK, E)
    tgt_norms = square_norms(group_pts).reshape(group_blocks, BLK)
    wt_blocks = group_wts.reshape(group_blocks, BLK, WCOL)
    skel_pts = jnp.take(points, skel_index.reshape(-1), axis=0).reshape(node_dev, RANK, E)
    panels = []
    for tree_level in range(LEVELS):
        first_node = level_start[tree_level]
        last_node = first_node + level_nodes[tree_level]
        lvl_pts, lvl_wts = (
            lax.all_gather(skel_pts[first_node:last_node], "tgt", axis=0, tiled=True),
            lax.all_gather(equiv_weights[first_node:last_node], "tgt", axis=0, tiled=True),
        )
        panels.append((lvl_pts, square_norms(lvl_pts), lvl_wts, level_nodes[tree_level], 0))
    own_blocks = points.reshape(blk_dev, BLK, E)
    own_norms = lax.dynamic_slice_in_dim(tgt_norms, src_index * blk_dev, blk_dev, 0)
    near_live = near_list >= 0
    near_index = jnp.where(near_live, near_list, 0)
    sources = tgt_blocks[near_index].reshape(blk_dev, NEAR * BLK, E)
    source_norms = tgt_norms[near_index].reshape(blk_dev, NEAR * BLK)
    source_wts = wt_blocks[near_index].reshape(blk_dev, NEAR * BLK, WCOL)
    kernel = tile_kernel(
        own_blocks, own_norms, sources, source_norms, jnp.repeat(near_live, BLK, axis=1)
    )
    own_near = apply_tile(kernel, source_wts).reshape(point_dev, WCOL)
    row_count = src_size * point_dev
    block_count = row_count // BLK
    far_total = jnp.zeros((block_count, BLK, WCOL), jnp.float32)
    for tree_level in range(LEVELS):
        panel_pts, panel_norms, panel_wts, stride_rows, offset_rows = panels[tree_level]
        level_count = level_nodes[tree_level]
        far_entry = far_list[:, tree_level, 0]
        far_live = far_entry >= 0
        far_entry = jnp.where(far_live, far_entry, 0)
        panel_rows = far_entry // level_count * stride_rows + offset_rows + far_entry % level_count
        kernel = tile_kernel(
            tgt_blocks,
            tgt_norms,
            panel_pts[panel_rows],
            panel_norms[panel_rows],
            jnp.broadcast_to(far_live[:, None], (block_count, RANK)),
        )
        far_total = far_total + apply_tile(kernel, panel_wts[panel_rows])
    whole_term = lax.psum(far_total.reshape(row_count, WCOL), "src")
    mine_term = lax.dynamic_slice_in_dim(whole_term, src_index * point_dev, point_dev, 0)
    mine_term = mine_term + own_near
    return mine_term


def solution(mesh):
    in_specs = (
        P(("tgt", "src"), None),
        P(("tgt", "src"), None),
        P(("tgt", "src"), None),
        P("tgt", None, "src"),
        P(("tgt", "src"), None),
        P(("tgt", "src"), None, None),
    )
    out_specs = P(("tgt", "src"), None)
    return jax.shard_map(shards, mesh=mesh, in_specs=in_specs, out_specs=out_specs, check_vma=False)
```

profile of v0, /device:TPU:0, one launch (start us, length us, event | category | flops | bytes accessed | tf_op | source)
XLA Modules:
  0.0 471.0 jit_solution(658145759099932878)
XLA Ops:
  6.6 1.6 slice.43
  8.2 0.7 all-gather.19.cloned.1.call-update
  9.0 0.7 reshape.304
  9.7 0.7 copy.36
  10.4 5.5 %gather_fusion = bf16[1792,256]{1,0:T(8,128)(2,1)S(1)} fusion(bf16[2048,256]{1,0:T(8,128)(2,1)} %param.6, s32[2048]{0:T(1024)S(1)} %pad_clamp_fusion), kind=kCustom, calls=%fused_computation | custom fusion | bytes 1842176 | tf_op jit(solution)/shard_map/jit(_take)/gather | solution.py:47
  16.0 0.3 broadcast_select_fusion
  16.3 0.7 slice.76
  17.0 0.7 slice.39
  17.8 0.7 slice.75
  18.6 0.5 all-gather.9.cloned.1.call-update
  19.2 0.8 slice.74
  20.1 0.1 reshape.395
  20.2 0.1 broadcast_in_dim.84
  20.4 26.1 %all_gather.30 = bf16[16,256,64]{1,2,0:T(8,128)(2,1)S(1)} all-gather(bf16[1,256,64]{1,2,0:T(8,128)(2,1)S(1)} %slice-done), channel_id=1, replica_groups=mesh['tgt'=16,'src'=8] {'tgt'}, dimensions={0}, use_global_device_ids=true | all-gather | bytes 557056 | tf_op jit(solution)/shard_map/all_gather | solution.py:54
  46.5 2.8 gather_fusion.9
  49.3 5.6 %all-gather.17.cloned.1.call-done = bf16[32,256,64]{1,2,0:T(8,128)(2,1)} async-done(((bf16[2,256,64]{1,2,0:T(8,128)(2,1)}), bf16[32,256,64]{1,2,0:T(8,128)(2,1)}) %all-gather.17.cloned.1.call-update) | async-done | bytes 1048592 | tf_op jit(solution)/shard_map/all_gather | solution.py:54
  54.9 4.0 gather_fusion.6
  58.9 22.5 %all-gather.19.cloned.1.call-done = bf16[16384,64]{0,1:T(8,128)(2,1)} async-done(((bf16[2048,64]{0,1:T(8,128)(2,1)}), bf16[16384,64]{0,1:T(8,128)(2,1)}) %all-gather.19.cloned.1.call-update) | async-done | bytes 2097168 | tf_op jit(solution)/shard_map/all_gather | solution.py:42
  81.4 2.2 copy_bitcast_fusion.1
  83.6 3.1 gather_fusion.12
  86.7 6.9 %copy.25 = bf16[256,128,64]{1,0,2:T(8,128)(2,1)} copy(bf16[256,128,64]{1,2,0:T(8,128)(2,1)} %gather_fusion.12) | data formatting | bytes 8388608 | tf_op jit(solution)/shard_map/gather | solution.py:63
  93.6 7.3 %reshape.311 = bf16[16,2048,64]{1,0,2:T(8,128)(2,1)} reshape(bf16[256,128,64]{1,0,2:T(8,128)(2,1)} %copy.25) | data formatting | bytes 8388608 | tf_op jit(solution)/shard_map/reshape | solution.py:63
  100.9 28.0 %all-gather.21.cloned.1.call-done = bf16[4096,256]{1,0:T(8,128)(2,1)} async-done(((bf16[256,256]{1,0:T(8,128)(2,1)}), bf16[4096,256]{1,0:T(8,128)(2,1)}) %all-gather.21.cloned.1.call-update) | async-done | bytes 2097168 | tf_op jit(solution)/shard_map/all_gather | solution.py:53
  128.9 10.0 %gather_fusion.8 = bf16[128,256,256]{2,1,0:T(8,128)(2,1)} fusion(bf16[16,256,256]{2,1,0:T(8,128)(2,1)} %bitcast.126, s32[1024]{0:T(1024)S(1)} %pad_clamp_fusion.2), kind=kCustom, calls=%fused_computation.8 | custom fusion | bytes 33554944 | tf_op jit(solution)/shard_map/gather | solution.py:81
  139.0 0.6 multiply_reduce_fusion.3
  139.6 0.8 gather_fusion.7
  140.3 34.9 %all-gather.13.cloned.1.call-done = bf16[64,256,64]{1,2,0:T(8,128)(2,1)} async-done(((bf16[4,256,64]{1,2,0:T(8,128)(2,1)}), bf16[64,256,64]{1,2,0:T(8,128)(2,1)}) %all-gather.13.cloned.1.call-update) | async-done | bytes 2097168 | tf_op jit(solution)/shard_map/all_gather | solution.py:54
  175.2 4.4 gather_fusion.3
  179.6 48.4 %all-gather.15.cloned.1.call-done = bf16[32,256,256]{2,1,0:T(8,128)(2,1)} async-done(((bf16[2,256,256]{2,1,0:T(8,128)(2,1)}), bf16[32,256,256]{2,1,0:T(8,128)(2,1)}) %all-gather.15.cloned.1.call-update) | async-done | bytes 4194320 | tf_op jit(solution)/shard_map/all_gather | solution.py:53
  228.0 3.3 multiply_reduce_fusion.2
  231.3 0.8 gather_fusion.4
  232.1 11.1 %gather_fusion.5 = bf16[128,256,256]{2,1,0:T(8,128)(2,1)} fusion(bf16[32,256,256]{2,1,0:T(8,128)(2,1)} %all-gather.15.cloned.1.call-done, s32[1024]{0:T(1024)S(1)} %pad_clamp_fusion.3), kind=kCustom, calls=%fused_computation.5 | custom fusion | bytes 33554944 | tf_op jit(solution)/shard_map/gather | solution.py:81
  243.2 35.7 %all-gather.9.cloned.1.call-done = bf16[16384,256]{1,0:T(8,128)(2,1)} async-done(((bf16[2048,256]{1,0:T(8,128)(2,1)}), bf16[16384,256]{1,0:T(8,128)(2,1)}) %all-gather.9.cloned.1.call-update) | async-done | bytes 8388624 | tf_op jit(solution)/shard_map/all_gather | solution.py:41
  278.8 5.2 %multiply_reduce_fusion.1 = f32[16384]{0:T(1024)S(1)} fusion(bf16[16384,256]{1,0:T(8,128)(2,1)} %all-gather.9.cloned.1.call-done), kind=kLoop, calls=%fused_computation.34 | loop fusion | flops 12566528 | bytes 8454144 | tf_op jit(solution)/shard_map/reduce_sum | solution.py:16
  284.1 0.7 gather_fusion.10
  284.8 12.8 %gather_fusion.11 = bf16[256,128,256]{2,1,0:T(8,128)(2,1)} fusion(bf16[128,128,256]{2,1,0:T(8,128)(2,1)} %bitcast.128, s32[1024]{0:T(1024)S(1)} %pad_clamp_fusion.1), kind=kCustom, calls=%fused_computation.11 | custom fusion | bytes 33555456 | tf_op jit(solution)/shard_map/gather | solution.py:61
  297.6 14.1 %fusion.16 = f32[128,128,64]{1,2,0:T(8,128)} fusion(bf16[128,256,64]{1,2,0:T(8,128)(2,1)} %gather_fusion.9, bf16[128,256,256]{2,1,0:T(8,128)(2,1)} %gather_fusion.8, bf16[128,128,256]{2,1,0:T(8,128)(2,1)} %bitcast.129, f32[128,256]{1,0:T(8,128)S(1)} %gather_fusion.7, f32[128,128]{1,0:T(8,128)S(1)} %bitcast.135, pred[128]{0:T(512)(128)(4,1)S(1)} %get-tuple-element.6), kind=kOutput, calls=%fused_computation.35 | convolution fusion | flops 2709520384 | bytes 33751168 | tf_op jit(solution)/shard_map/bis,bsw->biw/dot_general | solution.py:28
  311.7 14.3 %fusion.17 = f32[128,128,64]{1,2,0:T(8,128)} fusion(bf16[128,256,64]{1,2,0:T(8,128)(2,1)} %gather_fusion.6, bf16[128,256,256]{2,1,0:T(8,128)(2,1)} %gather_fusion.5, bf16[128,128,256]{2,1,0:T(8,128)(2,1)} %bitcast.130, f32[128,256]{1,0:T(8,128)S(1)} %gather_fusion.4, f32[128,128]{1,0:T(8,128)S(1)} %bitcast.136, pred[128]{0:T(512)(128)(4,1)S(1)} %get-tuple-element.7), kind=kOutput, calls=%fused_computation.36 | convolution fusion | flops 2709520384 | bytes 33751168 | tf_op jit(solution)/shard_map/bis,bsw->biw/dot_general | solution.py:28
  326.0 26.1 %all-gather.11.cloned.1.call-done = bf16[64,256,256]{2,1,0:T(8,128)(2,1)} async-done(((bf16[4,256,256]{2,1,0:T(8,128)(2,1)}), bf16[64,256,256]{2,1,0:T(8,128)(2,1)}) %all-gather.11.cloned.1.call-update) | async-done | bytes 8388624 | tf_op jit(solution)/shard_map/all_gather | solution.py:53
  352.1 5.6 %multiply_reduce_fusion = f32[64,256]{1,0:T(8,128)S(1)} fusion(bf16[64,256,256]{2,1,0:T(8,128)(2,1)} %all-gather.11.cloned.1.call-done), kind=kLoop, calls=%fused_computation.33 | loop fusion | flops 12566528 | bytes 8454144 | tf_op jit(solution)/shard_map/reduce_sum | solution.py:16
  357.7 0.8 gather_fusion.1
  358.5 11.6 %gather_fusion.2 = bf16[128,256,256]{2,1,0:T(8,128)(2,1)} fusion(bf16[64,256,256]{2,1,0:T(8,128)(2,1)} %all-gather.11.cloned.1.call-done, s32[1024]{0:T(1024)S(1)} %pad_clamp_fusion.4), kind=kCustom, calls=%fused_computation.2 | custom fusion | bytes 33554944 | tf_op jit(solution)/shard_map/gather | solution.py:81
  370.1 15.5 %add_bitcast_fusion = f32[128,8,8,128]{3,2,1,0:T(8,128)} fusion(f32[128,128,64]{1,2,0:T(8,128)} %fusion.16, f32[128,128,64]{1,2,0:T(8,128)} %fusion.17, bf16[128,256,64]{1,2,0:T(8,128)(2,1)} %gather_fusion.3, bf16[128,256,256]{2,1,0:T(8,128)(2,1)} %gather_fusion.2, bf16[128,128,256]{2,1,0:T(8,128)(2,1)} %bitcast.131, f32[128,256]{1,0:T(8,128)S(1)} %gather_fusion.1, ...), kind=kOutput, calls=%fused_computation.62 | convolution fusion | flops 2711617536 | bytes 42139776 | tf_op jit(solution)/shard_map/bis,bsw->biw/dot_general | solution.py:28
  385.7 4.5 copy.47
  390.2 12.0 %fusion.87 = bf16[16,128,2048]{1,2,0:T(8,128)(2,1)S(1)} fusion(f32[16,2048]{1,0:T(8,128)S(1)} %add.225, f32[16,128]{1,0:T(8,128)S(1)} %constant_dynamic-slice_fusion, pred[16,2048]{1,0:T(8,128)(4,1)S(1)} %bitcast.143, bf16[16,2048,256]{2,1,0:T(8,128)(2,1)} %bitcast.138, bf16[16,128,256]{2,1,0:T(8,128)(2,1)S(1)} %bitcast.132), kind=kOutput, calls=%fused_computation.17.clone.clone.clone.clone.1 | convolution fusion | flops 2172649472 | bytes 26386432 | tf_op jit(solution)/shard_map/bie,bse->bis/dot_general | solution.py:20
  402.2 5.0 %fusion.43 = f32[16,8,8,128]{3,2,1,0:T(8,128)S(1)} fusion(bf16[16,2048,64]{1,0,2:T(8,128)(2,1)S(1)} %copy-done.2, bf16[16,128,2048]{1,2,0:T(8,128)(2,1)S(1)} %fusion.87), kind=kOutput, calls=%fused_computation.65 | convolution fusion | flops 536870912 | bytes 13107200 | tf_op jit(solution)/shard_map/bis,bsw->biw/dot_general | solution.py:28
  407.2 55.1 %all-reduce.2.cloned.1.call-done = f32[16384,64]{0,1:T(8,128)} async-done(((f32[16384,64]{0,1:T(8,128)}), f32[16384,64]{0,1:T(8,128)}) %all-reduce.2.cloned.1.call-update) | async-done | bytes 4194320 | tf_op jit(solution)/shard_map/psum | solution.py:86
  462.3 1.9 bitcast_add_fusion
  (42 shorter events, 0.6 us)
Async XLA Ops:
  6.5 10.5 %copy-start.3 = (bf16[7,256,64]{1,2,0:T(8,128)(2,1)S(1)}, bf16[7,256,64]{1,2,0:T(8,128)(2,1)}, u32[]{:S(2)}) copy-start(bf16[7,256,64]{1,2,0:T(8,128)(2,1)} %param.11) | copy-start | bytes 688132
  6.5 13.8 %slice-start = ((bf16[7,256,64]{1,2,0:T(8,128)(2,1)}), bf16[1,256,64]{1,2,0:T(8,128)(2,1)S(1)}, s32[]{:S(2)}) async-start(bf16[7,256,64]{1,2,0:T(8,128)(2,1)} %param.11), calls=%async_computation.8 | async-start | bytes 65536 | tf_op jit(solution)/shard_map/slice | solution.py:54
  6.5 13.5 %copy-start.4 = (s32[16,16]{1,0:T(8,128)S(1)}, s32[16,16]{1,0:T(8,128)}, u32[]{:S(2)}) copy-start(s32[16,16]{1,0:T(8,128)} %param.8) | copy-start | bytes 3076
  6.5 13.8 %copy-start.5 = (s32[128,3,1]{0,2,1:T(1,128)S(1)}, s32[128,3,1]{0,2,1:T(1,128)}, u32[]{:S(2)}) copy-start(s32[128,3,1]{0,2,1:T(1,128)} %param.9) | copy-start | bytes 4612
  6.5 48.4 %all-gather.17.cloned.1.call-start = ((), (), s32[]{:S(2)}) async-start(), calls=%async_computation.4 | async-start | bytes 1114112 | tf_op jit(solution)/shard_map/all_gather | solution.py:54
  8.2 73.2 %all-gather.19.cloned.1.call-start = ((), (), s32[]{:S(2)}) async-start(), calls=%async_computation.6 | async-start | bytes 2359296 | tf_op jit(solution)/shard_map/all_gather | solution.py:42
  8.9 120.0 %all-gather.21.cloned.1.call-start = ((), (), s32[]{:S(2)}) async-start(), calls=%async_computation.7 | async-start | bytes 2228224 | tf_op jit(solution)/shard_map/all_gather | solution.py:53
  17.0 158.2 %all-gather.13.cloned.1.call-start = ((), (), s32[]{:S(2)}) async-start(), calls=%async_computation.2 | async-start | bytes 2228224 | tf_op jit(solution)/shard_map/all_gather | solution.py:54
  17.7 210.3 %all-gather.15.cloned.1.call-start = ((), (), s32[]{:S(2)}) async-start(), calls=%async_computation.3 | async-start | bytes 4456448 | tf_op jit(solution)/shard_map/all_gather | solution.py:53
  18.6 260.3 %all-gather.9.cloned.1.call-start = ((), (), s32[]{:S(2)}) async-start(), calls=%async_computation | async-start | bytes 9437184 | tf_op jit(solution)/shard_map/all_gather | solution.py:41
  19.1 333.0 %all-gather.11.cloned.1.call-start = ((), (), s32[]{:S(2)}) async-start(), calls=%async_computation.1 | async-start | bytes 8912896 | tf_op jit(solution)/shard_map/all_gather | solution.py:53
  20.0 442.3 %all-reduce.2.cloned.1.call-start = ((), (), s32[]{:S(2)}) async-start(), calls=%async_computation.5 | async-start | bytes 8388608 | tf_op jit(solution)/shard_map/psum | solution.py:86
  128.9 10.0 %copy-start = (bf16[4096,256]{1,0:T(8,128)(2,1)S(1)}, bf16[4096,256]{1,0:T(8,128)(2,1)}, u32[]{:S(2)}) copy-start(bf16[4096,256]{1,0:T(8,128)(2,1)} %all-gather.21.cloned.1.call-done) | copy-start | bytes 6291460
  385.7 4.5 copy-start.1
  390.2 12.0 %copy-start.2 = (bf16[16,2048,64]{1,0,2:T(8,128)(2,1)S(1)}, bf16[16,2048,64]{1,0,2:T(8,128)(2,1)}, u32[]{:S(2)}) copy-start(bf16[16,2048,64]{1,0,2:T(8,128)(2,1)} %reshape.311) | copy-start | bytes 12582916
Sparse Core Ops, SparseCore 0:
  9.5 45.4 all-gather.16
  56.6 24.7 all-gather.18
  83.6 45.3 all-gather.20
  130.9 44.2 all-gather.12
  177.2 50.7 all-gather.14
  229.6 49.2 all-gather.8
  281.0 71.0 all-gather.10
  390.3 71.9 all-reduce.1
where the time goes:
time: 472 us; the launch traced here: 471 us
  waiting for transfers between devices  257 us (54%)
  local copies, waits for them, and re-layouts  95.4 us (20%)
  matrix products  60.9 us (13%)
  blocking collectives  26.1 us (6%)
  other arithmetic  17.1 us (4%)
  between operations  13.7 us (3%)
    all_gather x3, waiting for transfers between devices, shards(): lax.all_gather(skel_pts[first_node:last_node], 'tgt', axis=0, tiled=True)  102 us
    psum x1, waiting for transfers between devices, shards(): whole_term = lax.psum(far_total.reshape(row_count, WCOL), 'src')  55.1 us
    dot_general x4, matrix products, apply_tile(): jnp.einsum('bis,bsw->biw', kernel, source_weights, preferred_element_type...  49 us
    all_gather x2, waiting for transfers between devices, shards(): lax.all_gather(equiv_weights[first_node:last_node], 'tgt', axis=0, tiled=...  40.5 us
    all_gather x1, waiting for transfers between devices, shards(): lax.all_gather(points, 'src', axis=0, tiled=True)  35.7 us
    gather x3, local copies, waits for them, and re-layouts, shards(): panel_pts[panel_rows]  32.8 us
    all_gather x1, blocking collectives, shards(): lax.all_gather(equiv_weights[first_node:last_node], 'tgt', axis=0, tiled=...  26.1 us
    all_gather x1, waiting for transfers between devices, shards(): lax.all_gather(weights, 'src', axis=0, tiled=True)  22.5 us
  transfers between devices with their start and end apart: 8, of which 8 were waited for; matrix products, arithmetic and copies ran while one was open for 28% of the time, Pallas kernels for 0%

commit v1 on v0

--- a/solution.py
+++ b/solution.py
@@ -38,7 +38,9 @@
     level_nodes = [blk_dev // (4 * 2**tree_level) for tree_level in range(LEVELS)]
     level_start = [sum(level_nodes[:tree_level]) for tree_level in range(LEVELS)]
     group_pts, group_wts = (
-        lax.all_gather(points, "src", axis=0, tiled=True),
+        jnp.concatenate(
+            lax.all_to_all(jnp.stack([points] * lax.axis_size("src")), "src", 0, 0), axis=0
+        ),
         lax.all_gather(weights, "src", axis=0, tiled=True),
     )
     tgt_blocks = group_pts.reshape(group_blocks, BLK, E)

time: 472 us -> 426 us (0.903)
  waiting for transfers between devices: 257 us -> 203 us
  starting transfers between devices: 0.32 us -> 5.34 us
    all_gather x1 -> x0, waiting for transfers between devices: 35.7 us -> none  [shards(): lax.all_gather(points, 'src', axis=0, tiled=True)]
    all_gather x3, waiting for transfers between devices: 102 us -> 86.1 us  [shards(): lax.all_gather(skel_pts[first_node:last_node], 'tgt', axis=0, tiled=True)]
    all_gather x2, waiting for transfers between devices: 40.5 us -> 34.9 us  [shards(): lax.all_gather(equiv_weights[first_node:last_node], 'tgt', axis=0, tiled=...]
    all_to_all x0 -> x1, starting transfers between devices: none -> 5.09 us  [shards(): lax.all_to_all(jnp.stack([points] * lax.axis_size('src')), 'src', 0, 0)]
  transfers between devices with their start and end apart: 8 -> 8, of which waited for: 8 -> 6; matrix products, arithmetic and copies ran while one was open for 28% -> 32% of each run, Pallas kernels for 0% -> 0%
where the time goes in v1:
time: 426 us; the launch traced here: 425 us
  waiting for transfers between devices  203 us (48%)
  local copies, waits for them, and re-layouts  98.4 us (23%)
  matrix products  61.1 us (14%)
  blocking collectives  26.1 us (6%)
  other arithmetic  17.5 us (4%)
  between operations  13.7 us (3%)
  starting transfers between devices  5.34 us (1%)
    all_gather x3, waiting for transfers between devices, shards(): lax.all_gather(skel_pts[first_node:last_node], 'tgt', axis=0, tiled=True)  86.1 us
    psum x1, waiting for transfers between devices, shards(): whole_term = lax.psum(far_total.reshape(row_count, WCOL), 'src')  54.7 us
    dot_general x4, matrix products, apply_tile(): jnp.einsum('bis,bsw->biw', kernel, source_weights, preferred_element_type...  48.8 us
    all_gather x2, waiting for transfers between devices, shards(): lax.all_gather(equiv_weights[first_node:last_node], 'tgt', axis=0, tiled=...  34.9 us
    gather x3, local copies, waits for them, and re-layouts, shards(): panel_pts[panel_rows]  32.1 us
    all_gather x1, waiting for transfers between devices, shards(): lax.all_gather(weights, 'src', axis=0, tiled=True)  26.2 us
    all_gather x1, blocking collectives, shards(): lax.all_gather(equiv_weights[first_node:last_node], 'tgt', axis=0, tiled=...  26.1 us
    reduce_sum x4, other arithmetic, square_norms(): return jnp.sum(jnp.square(values.astype(jnp.float32)), axis=-1)  15.2 us
  transfers between devices with their start and end apart: 8, of which 6 were waited for; matrix products, arithmetic and copies ran while one was open for 32% of the time, Pallas kernels for 0%

profile of v1, /device:TPU:0, one launch (start us, length us, event | category | flops | bytes accessed | tf_op | source)
XLA Modules:
  0.0 424.9 jit_solution(10718558688229748043)
XLA Ops:
  6.5 1.6 slice.43
  8.2 0.7 all-gather.16.cloned.1.call-update
  8.9 0.7 reshape.307
  9.6 0.7 copy.36
  10.4 5.5 %gather_fusion = bf16[1792,256]{1,0:T(8,128)(2,1)S(1)} fusion(bf16[2048,256]{1,0:T(8,128)(2,1)} %param.6, s32[2048]{0:T(1024)S(1)} %pad_clamp_fusion), kind=kCustom, calls=%fused_computation | custom fusion | bytes 1842176 | tf_op jit(solution)/shard_map/jit(_take)/gather | solution.py:49
  15.9 0.3 broadcast_select_fusion
  16.2 0.7 slice.76
  17.0 0.7 slice.39
  17.7 0.7 slice.75
  18.5 0.8 slice.74
  19.4 3.8 stack.2
  23.1 5.1 %all-to-all-start = ((bf16[8,2048,256]{2,1,0:T(8,128)(2,1)}), bf16[8,2048,256]{2,1,0:T(8,128)(2,1)}, u32[]{:S(2)}, u32[]{:S(2)}) async-start(bf16[8,2048,256]{2,1,0:T(8,128)(2,1)} %stack.2), calls=%async_computation | async-start | bytes 16777216 | tf_op jit(solution)/shard_map/all_to_all | solution.py:42
  28.3 0.0 all-reduce.2.cloned.1.call-start
  28.3 0.1 reshape.397
  28.4 0.1 broadcast_in_dim.84
  28.6 26.1 %all_gather.26 = bf16[16,256,64]{1,2,0:T(8,128)(2,1)S(1)} all-gather(bf16[1,256,64]{1,2,0:T(8,128)(2,1)S(1)} %slice-done), channel_id=1, replica_groups=mesh['tgt'=16,'src'=8] {'tgt'}, dimensions={0}, use_global_device_ids=true | all-gather | bytes 557056 | tf_op jit(solution)/shard_map/all_gather | solution.py:56
  54.7 2.8 gather_fusion.9
  57.5 4.0 gather_fusion.6
  61.5 26.2 %all-gather.16.cloned.1.call-done = bf16[16384,64]{0,1:T(8,128)(2,1)} async-done(((bf16[2048,64]{0,1:T(8,128)(2,1)}), bf16[16384,64]{0,1:T(8,128)(2,1)}) %all-gather.16.cloned.1.call-update) | async-done | bytes 2097168 | tf_op jit(solution)/shard_map/all_gather | solution.py:44
  87.7 2.2 copy_bitcast_fusion.1
  89.9 3.1 gather_fusion.12
  93.0 6.8 %copy.25 = bf16[256,128,64]{1,0,2:T(8,128)(2,1)} copy(bf16[256,128,64]{1,2,0:T(8,128)(2,1)} %gather_fusion.12) | data formatting | bytes 8388608 | tf_op jit(solution)/shard_map/gather | solution.py:65
  99.9 7.3 %reshape.313 = bf16[16,2048,64]{1,0,2:T(8,128)(2,1)} reshape(bf16[256,128,64]{1,0,2:T(8,128)(2,1)} %copy.25) | data formatting | bytes 8388608 | tf_op jit(solution)/shard_map/reshape | solution.py:65
  107.2 27.5 %all-gather.18.cloned.1.call-done = bf16[4096,256]{1,0:T(8,128)(2,1)} async-done(((bf16[256,256]{1,0:T(8,128)(2,1)}), bf16[4096,256]{1,0:T(8,128)(2,1)}) %all-gather.18.cloned.1.call-update) | async-done | bytes 2097168 | tf_op jit(solution)/shard_map/all_gather | solution.py:55
  134.7 10.0 %gather_fusion.8 = bf16[128,256,256]{2,1,0:T(8,128)(2,1)} fusion(bf16[16,256,256]{2,1,0:T(8,128)(2,1)} %bitcast.125, s32[1024]{0:T(1024)S(1)} %pad_clamp_fusion.2), kind=kCustom, calls=%fused_computation.8 | custom fusion | bytes 33554944 | tf_op jit(solution)/shard_map/gather | solution.py:83
  144.7 0.6 multiply_reduce_fusion.3
  145.3 0.8 gather_fusion.7
  146.1 34.9 %all-gather.10.cloned.1.call-done = bf16[64,256,64]{1,2,0:T(8,128)(2,1)} async-done(((bf16[4,256,64]{1,2,0:T(8,128)(2,1)}), bf16[64,256,64]{1,2,0:T(8,128)(2,1)}) %all-gather.10.cloned.1.call-update) | async-done | bytes 2097168 | tf_op jit(solution)/shard_map/all_gather | solution.py:56
  181.0 4.4 %gather_fusion.3 = bf16[128,256,64]{1,2,0:T(8,128)(2,1)} fusion(bf16[64,256,64]{1,2,0:T(8,128)(2,1)} %all-gather.10.cloned.1.call-done, s32[1024]{0:T(1024)S(1)} %pad_clamp_fusion.4), kind=kCustom, calls=%fused_computation.3 | custom fusion | bytes 8389120 | tf_op jit(solution)/shard_map/gather | solution.py:87
  185.4 5.6 %multiply_reduce_fusion.1 = f32[8,2048]{1,0:T(8,128)S(1)} fusion(bf16[8,2048,256]{2,1,0:T(8,128)(2,1)} %all-to-all-done), kind=kLoop, calls=%fused_computation.34 | loop fusion | flops 12566528 | bytes 8454144 | tf_op jit(solution)/shard_map/reduce_sum | solution.py:16
  191.1 0.7 gather_fusion.10
  191.8 12.9 %gather_fusion.11 = bf16[256,128,256]{2,1,0:T(8,128)(2,1)} fusion(bf16[128,128,256]{2,1,0:T(8,128)(2,1)} %bitcast.4, s32[1024]{0:T(1024)S(1)} %pad_clamp_fusion.1), kind=kCustom, calls=%fused_computation.11 | custom fusion | bytes 33555456 | tf_op jit(solution)/shard_map/gather | solution.py:63
  204.8 14.3 %fusion.16 = f32[128,128,64]{1,2,0:T(8,128)} fusion(bf16[128,256,64]{1,2,0:T(8,128)(2,1)} %gather_fusion.9, bf16[128,256,256]{2,1,0:T(8,128)(2,1)} %gather_fusion.8, bf16[128,128,256]{2,1,0:T(8,128)(2,1)} %bitcast.4, f32[128,256]{1,0:T(8,128)S(1)} %gather_fusion.7, f32[128,128]{1,0:T(8,128)S(1)} %add.200, pred[128]{0:T(512)(128)(4,1)S(1)} %get-tuple-element.6), kind=kOutput, calls=%fused_computation.35 | convolution fusion | flops 2709520384 | bytes 33751168 | tf_op jit(solution)/shard_map/bis,bsw->biw/dot_general | solution.py:28
  219.0 14.7 %all-gather.12.cloned.1.call-done = bf16[32,256,256]{2,1,0:T(8,128)(2,1)} async-done(((bf16[2,256,256]{2,1,0:T(8,128)(2,1)}), bf16[32,256,256]{2,1,0:T(8,128)(2,1)}) %all-gather.12.cloned.1.call-update) | async-done | bytes 4194320 | tf_op jit(solution)/shard_map/all_gather | solution.py:55
  233.8 3.3 multiply_reduce_fusion.2
  237.1 0.8 gather_fusion.4
  237.9 10.5 %gather_fusion.5 = bf16[128,256,256]{2,1,0:T(8,128)(2,1)} fusion(bf16[32,256,256]{2,1,0:T(8,128)(2,1)} %all-gather.12.cloned.1.call-done, s32[1024]{0:T(1024)S(1)} %pad_clamp_fusion.3), kind=kCustom, calls=%fused_computation.5 | custom fusion | bytes 33554944 | tf_op jit(solution)/shard_map/gather | solution.py:83
  248.4 14.1 %fusion.17 = f32[128,128,64]{1,2,0:T(8,128)} fusion(bf16[128,256,64]{1,2,0:T(8,128)(2,1)} %gather_fusion.6, bf16[128,256,256]{2,1,0:T(8,128)(2,1)} %gather_fusion.5, bf16[128,128,256]{2,1,0:T(8,128)(2,1)} %bitcast.4, f32[128,256]{1,0:T(8,128)S(1)} %gather_fusion.4, f32[128,128]{1,0:T(8,128)S(1)} %add.200, pred[128]{0:T(512)(128)(4,1)S(1)} %get-tuple-element.7), kind=kOutput, calls=%fused_computation.36 | convolution fusion | flops 2709520384 | bytes 33751168 | tf_op jit(solution)/shard_map/bis,bsw->biw/dot_general | solution.py:28
  262.4 43.9 %all-gather.8.cloned.1.call-done = bf16[64,256,256]{2,1,0:T(8,128)(2,1)} async-done(((bf16[4,256,256]{2,1,0:T(8,128)(2,1)}), bf16[64,256,256]{2,1,0:T(8,128)(2,1)}) %all-gather.8.cloned.1.call-update) | async-done | bytes 8388624 | tf_op jit(solution)/shard_map/all_gather | solution.py:55
  306.3 5.6 %multiply_reduce_fusion = f32[64,256]{1,0:T(8,128)S(1)} fusion(bf16[64,256,256]{2,1,0:T(8,128)(2,1)} %all-gather.8.cloned.1.call-done), kind=kLoop, calls=%fused_computation.33 | loop fusion | flops 12566528 | bytes 8454144 | tf_op jit(solution)/shard_map/reduce_sum | solution.py:16
  312.0 0.8 gather_fusion.1
  312.7 11.6 %gather_fusion.2 = bf16[128,256,256]{2,1,0:T(8,128)(2,1)} fusion(bf16[64,256,256]{2,1,0:T(8,128)(2,1)} %all-gather.8.cloned.1.call-done, s32[1024]{0:T(1024)S(1)} %pad_clamp_fusion.4), kind=kCustom, calls=%fused_computation.2 | custom fusion | bytes 33554944 | tf_op jit(solution)/shard_map/gather | solution.py:83
  324.3 15.4 %add_bitcast_fusion = f32[128,8,8,128]{3,2,1,0:T(8,128)} fusion(f32[128,128,64]{1,2,0:T(8,128)} %fusion.16, f32[128,128,64]{1,2,0:T(8,128)} %fusion.17, bf16[128,256,64]{1,2,0:T(8,128)(2,1)} %gather_fusion.3, bf16[128,256,256]{2,1,0:T(8,128)(2,1)} %gather_fusion.2, bf16[128,128,256]{2,1,0:T(8,128)(2,1)} %bitcast.4, f32[128,256]{1,0:T(8,128)S(1)} %gather_fusion.1, ...), kind=kOutput, calls=%fused_computation.62 | convolution fusion | flops 2711617536 | bytes 42139776 | tf_op jit(solution)/shard_map/bis,bsw->biw/dot_general | solution.py:28
  339.8 4.4 %copy.47 = f32[128,8,8,128]{3,2,0,1:T(8,128)} copy(f32[128,8,8,128]{3,2,1,0:T(8,128)} %add_bitcast_fusion) | data formatting | bytes 8388608 | tf_op jit(solution)/shard_map/reshape | solution.py:88
  344.2 12.2 %fusion.87 = bf16[16,128,2048]{1,2,0:T(8,128)(2,1)S(1)} fusion(f32[16,2048]{1,0:T(8,128)S(1)} %add.225, f32[16,128]{1,0:T(8,128)S(1)} %constant_dynamic-slice_fusion, pred[16,2048]{1,0:T(8,128)(4,1)S(1)} %bitcast.133, bf16[16,2048,256]{2,1,0:T(8,128)(2,1)} %bitcast.128, bf16[16,128,256]{2,1,0:T(8,128)(2,1)S(1)} %bitcast.127), kind=kOutput, calls=%fused_computation.17.clone.clone.clone.clone.1 | convolution fusion | flops 2172649472 | bytes 26386432 | tf_op jit(solution)/shard_map/bie,bse->bis/dot_general | solution.py:20
  356.4 5.0 %fusion.43 = f32[16,8,8,128]{3,2,1,0:T(8,128)S(1)} fusion(bf16[16,2048,64]{1,0,2:T(8,128)(2,1)S(1)} %copy-done.2, bf16[16,128,2048]{1,2,0:T(8,128)(2,1)S(1)} %fusion.87), kind=kOutput, calls=%fused_computation.65 | convolution fusion | flops 536870912 | bytes 13107200 | tf_op jit(solution)/shard_map/bis,bsw->biw/dot_general | solution.py:28
  361.5 54.7 %all-reduce.2.cloned.1.call-done = f32[16384,64]{0,1:T(8,128)} async-done(((f32[16384,64]{0,1:T(8,128)}), f32[16384,64]{0,1:T(8,128)}) %all-reduce.2.cloned.1.call-update) | async-done | bytes 4194320 | tf_op jit(solution)/shard_map/psum | solution.py:88
  416.2 1.9 bitcast_add_fusion
  (43 shorter events, 0.5 us)
Async XLA Ops:
  6.5 10.4 %copy-start.3 = (bf16[7,256,64]{1,2,0:T(8,128)(2,1)S(1)}, bf16[7,256,64]{1,2,0:T(8,128)(2,1)}, u32[]{:S(2)}) copy-start(bf16[7,256,64]{1,2,0:T(8,128)(2,1)} %param.11) | copy-start | bytes 688132
  6.5 12.8 %copy-start.1 = (bf16[2048,256]{1,0:T(8,128)(2,1)S(1)}, bf16[2048,256]{1,0:T(8,128)(2,1)}, u32[]{:S(2)}) copy-start(bf16[2048,256]{1,0:T(8,128)(2,1)} %param.6) | copy-start | bytes 3145732
  6.5 51.0 %all-gather.14.cloned.1.call-start = ((), (), s32[]{:S(2)}) async-start(), calls=%async_computation.4 | async-start | bytes 1114112 | tf_op jit(solution)/shard_map/all_gather | solution.py:56
  8.1 79.6 %all-gather.16.cloned.1.call-start = ((), (), s32[]{:S(2)}) async-start(), calls=%async_computation.6 | async-start | bytes 2359296 | tf_op jit(solution)/shard_map/all_gather | solution.py:44
  8.9 125.8 %all-gather.18.cloned.1.call-start = ((), (), s32[]{:S(2)}) async-start(), calls=%async_computation.7 | async-start | bytes 2228224 | tf_op jit(solution)/shard_map/all_gather | solution.py:55
  16.9 164.1 %all-gather.10.cloned.1.call-start = ((), (), s32[]{:S(2)}) async-start(), calls=%async_computation.2 | async-start | bytes 2228224 | tf_op jit(solution)/shard_map/all_gather | solution.py:56
  17.7 216.1 %all-gather.12.cloned.1.call-start = ((), (), s32[]{:S(2)}) async-start(), calls=%async_computation.3 | async-start | bytes 4456448 | tf_op jit(solution)/shard_map/all_gather | solution.py:55
  18.5 287.9 %all-gather.8.cloned.1.call-start = ((), (), s32[]{:S(2)}) async-start(), calls=%async_computation.1 | async-start | bytes 8912896 | tf_op jit(solution)/shard_map/all_gather | solution.py:55
  23.1 5.2 %copy-start.4 = (s32[16,16]{1,0:T(8,128)S(1)}, s32[16,16]{1,0:T(8,128)}, u32[]{:S(2)}) copy-start(s32[16,16]{1,0:T(8,128)} %param.8) | copy-start | bytes 3076
  23.1 5.4 %copy-start.5 = (s32[128,3,1]{0,2,1:T(1,128)S(1)}, s32[128,3,1]{0,2,1:T(1,128)}, u32[]{:S(2)}) copy-start(s32[128,3,1]{0,2,1:T(1,128)} %param.9) | copy-start | bytes 4612
  23.1 5.5 %slice-start = ((bf16[7,256,64]{1,2,0:T(8,128)(2,1)}), bf16[1,256,64]{1,2,0:T(8,128)(2,1)S(1)}, s32[]{:S(2)}) async-start(bf16[7,256,64]{1,2,0:T(8,128)(2,1)} %param.11), calls=%async_computation.8 | async-start | bytes 65536 | tf_op jit(solution)/shard_map/slice | solution.py:56
  23.1 162.3 %all-to-all-start = ((bf16[8,2048,256]{2,1,0:T(8,128)(2,1)}), bf16[8,2048,256]{2,1,0:T(8,128)(2,1)}, u32[]{:S(2)}, u32[]{:S(2)}) async-start(bf16[8,2048,256]{2,1,0:T(8,128)(2,1)} %stack.2), calls=%async_computation | async-start | bytes 16777216 | tf_op jit(solution)/shard_map/all_to_all | solution.py:42
  28.3 388.0 %all-reduce.2.cloned.1.call-start = ((), (), s32[]{:S(2)}) async-start(), calls=%async_computation.5 | async-start | bytes 8388608 | tf_op jit(solution)/shard_map/psum | solution.py:88
  134.7 10.0 %copy-start = (bf16[4096,256]{1,0:T(8,128)(2,1)S(1)}, bf16[4096,256]{1,0:T(8,128)(2,1)}, u32[]{:S(2)}) copy-start(bf16[4096,256]{1,0:T(8,128)(2,1)} %all-gather.18.cloned.1.call-done) | copy-start | bytes 6291460
  344.2 12.3 %copy-start.2 = (bf16[16,2048,64]{1,0,2:T(8,128)(2,1)S(1)}, bf16[16,2048,64]{1,0,2:T(8,128)(2,1)}, u32[]{:S(2)}) copy-start(bf16[16,2048,64]{1,0,2:T(8,128)(2,1)} %reshape.313) | copy-start | bytes 12582916
Sparse Core Ops, SparseCore 0:
  9.5 45.6 all-gather.13
  56.9 30.7 all-gather.15
  89.8 44.8 all-gather.17
  136.7 44.2 all-gather.9
  183.0 50.7 all-gather.11
  235.8 70.5 all-gather.7
  344.3 71.8 all-reduce.1
